TPU v7x, 32 devices: a whole 2x2x4 slice. The times are simulated.
32 devices in a mesh: space: 16 (over z, y, core), filt: 2 (over x).
Axes of the slice: x: 2, y: 2, z: 4, core: 2. Of those that a mesh axis runs over, the one named last changes fastest.
Arguments:
- volume: bfloat16 [64, 32, 4, 256], P(None, 'space', 'filt'), may hold values from -6 to 6
- first_weight: bfloat16 [27, 64, 64], replicated, may hold values from -0.15625 to 0.15625
- second_weight: bfloat16 [27, 128, 64], P(None, 'filt'), may hold values from -0.15625 to 0.15625
- cotangent: bfloat16 [128, 16, 2, 128], P('filt', 'space'), may hold values from -24 to 24
Outputs:
- features: bfloat16 [128, 16, 2, 128], P('filt', 'space')
- volume_grad: bfloat16 [64, 32, 4, 256], P(None, 'space', 'filt')
- first_grad: float32 [27, 64, 64], replicated
- second_grad: float32 [27, 128, 64], P(None, 'filt')
All inputs are finite; a program needn't handle non-finite values.
Results may differ from a plain program's by a relative error of at most 0.019.
Values may be sent and summed in bfloat16 or wider, within the bound.
No kernel may reach another device: no remote copies, remote signals or barrier semaphores. Data moves between devices by JAX's collectives and lax.ppermute only.
A program may use at most 64 MiB of HBM per device.

v0:
```python
import jax
import jax.numpy as jnp
from jax import lax
from jax.sharding import PartitionSpec as P


def extended(cells, sides, width):
    for axis, dim in sides:
        count = lax.axis_size(axis)
        ends = count - 1
        head = lax.slice_in_dim(cells, 0, width, axis=dim)
        tail = lax.slice_in_dim(cells, cells.shape[dim] - width, cells.shape[dim], axis=dim)
        cells = jnp.concatenate(
            [
                lax.ppermute(tail, axis, [(i, (i + 1) % count) for i in range(ends)]),
                cells,
                lax.ppermute(head, axis, [((i + 1) % count, i) for i in range(ends)]),
            ],
            axis=dim,
        )
    return cells


def silu_slope(values):
    sigmoid_part = jax.nn.sigmoid(values)
    return sigmoid_part * (1.0 + values * (1.0 - sigmoid_part))


def pad_depth(volume_field):
    return jnp.pad(volume_field, ((0, 0), (0, 0), (0, 0), (1, 1)))


def window(padded, offset_x, offset_y, offset_z, extents):
    extent_x, extent_y, extent_z = extents
    section = lax.slice(
        padded,
        (0, offset_x, offset_y, offset_z),
        (padded.shape[0], offset_x + extent_x, offset_y + extent_y, offset_z + extent_z),
    )
    return section.reshape(padded.shape[0], extent_x * extent_y * extent_z)


def conv_forward(padded, weight, extents):
    outputs, inputs = (weight.shape[1], weight.shape[2])
    running = jnp.zeros((outputs, extents[0] * extents[1] * extents[2]), jnp.float32)
    for offset_x in range(3):
        for offset_y in range(3):
            tap_base = offset_x * 9 + offset_y * 3
            stacked = jnp.concatenate(
                [window(padded, offset_x, offset_y, offset_z, extents) for offset_z in range(3)],
                axis=0,
            )
            matrices = jnp.transpose(weight[tap_base : tap_base + 3], (1, 0, 2)).reshape(
                outputs, 3 * inputs
            )
            running = running + jnp.dot(matrices, stacked, preferred_element_type=jnp.float32)
    return running


def conv_transpose(padded, weight, extents):
    outputs, inputs = (weight.shape[1], weight.shape[2])
    running = jnp.zeros((inputs, extents[0] * extents[1] * extents[2]), jnp.float32)
    for offset_x in range(3):
        for offset_y in range(3):
            tap_base = offset_x * 9 + offset_y * 3
            stacked = jnp.concatenate(
                [window(padded, offset_x, offset_y, offset_z, extents) for offset_z in range(3)],
                axis=0,
            )
            tap_block = weight[24 - tap_base : 27 - tap_base][::-1]
            matrices = jnp.transpose(tap_block, (2, 0, 1)).reshape(inputs, 3 * outputs)
            running = running + jnp.dot(matrices, stacked, preferred_element_type=jnp.float32)
    return running


def conv_weights(grad_rows, padded, extents):
    outputs, inputs = (grad_rows.shape[0], padded.shape[0])
    blocks = []
    for offset_x in range(3):
        for offset_y in range(3):
            stacked = jnp.concatenate(
                [window(padded, offset_x, offset_y, offset_z, extents) for offset_z in range(3)],
                axis=0,
            )
            section = lax.dot_general(
                grad_rows, stacked, (((1,), (1,)), ((), ())), preferred_element_type=jnp.float32
            )
            blocks.append(jnp.transpose(section.reshape(outputs, 3, inputs), (1, 0, 2)))
    return jnp.concatenate(blocks, axis=0)


def pool_cells(hidden):
    channels, size_x, size_y, size_z = hidden.shape
    pair_table = (jnp.arange(size_z)[:, None] // 2 == jnp.arange(size_z // 2)[None, :]).astype(
        jnp.bfloat16
    )
    depth_sums = jnp.dot(hidden.reshape(-1, size_z), pair_table, preferred_element_type=jnp.float32)
    depth_sums = depth_sums.reshape(channels, size_x // 2, 2, size_y // 2, 2, size_z // 2)
    return (0.125 * depth_sums.sum(axis=(2, 4))).astype(jnp.bfloat16)


def spread_cells(grad_field):
    scaled = 0.125 * grad_field
    scaled = jnp.repeat(scaled, 2, axis=1)
    scaled = jnp.repeat(scaled, 2, axis=2)
    return jnp.repeat(scaled, 2, axis=3)


def local(volume, first_weight, second_weight, cotangent):
    count_space = lax.axis_size("space")
    count_filt = lax.axis_size("filt")
    channels = volume.shape[0]
    fine_shape = volume.shape[1:]
    fine_cells = fine_shape[0] * fine_shape[1] * fine_shape[2] * count_space * count_filt
    fine_scale = 1.0 / fine_cells**0.5
    padded_in = pad_depth(extended(volume, (("space", 1), ("filt", 2)), 1))
    first_pre = conv_forward(padded_in, first_weight, fine_shape)
    hidden = jax.nn.silu(first_pre).astype(jnp.bfloat16).reshape((channels,) + fine_shape)
    pooled = pool_cells(hidden)
    brick_shape = pooled.shape[1:]
    brick_cells = brick_shape[0] * brick_shape[1] * brick_shape[2]
    bottom_scale = 1.0 / (brick_cells * count_space * count_filt) ** 0.5
    filters = second_weight.shape[1]
    whole_weight = lax.all_gather(second_weight, "filt", axis=1, tiled=True)
    total_filters = whole_weight.shape[1]
    padded_pool = pad_depth(extended(pooled, (("space", 1), ("filt", 2)), 1))
    second_pre = conv_forward(padded_pool, whole_weight, brick_shape)
    local_out = jax.nn.silu(second_pre).astype(jnp.bfloat16).reshape((total_filters,) + brick_shape)
    features = lax.all_to_all(local_out, "filt", split_axis=0, concat_axis=2, tiled=True)
    local_cot = lax.all_to_all(cotangent, "filt", split_axis=2, concat_axis=0, tiled=True)
    down_grad = (
        local_cot.reshape(total_filters, -1).astype(jnp.float32) * silu_slope(second_pre)
    ).astype(jnp.bfloat16)
    summed = lax.psum(conv_weights(down_grad, padded_pool, brick_shape), ("space", "filt"))
    second_grad = (
        lax.dynamic_slice_in_dim(summed, lax.axis_index("filt") * filters, filters, 1)
        * bottom_scale
    )
    padded_down = pad_depth(
        extended(down_grad.reshape((total_filters,) + brick_shape), (("space", 1), ("filt", 2)), 1)
    )

    def add_group(group_index, running):
        group_rows = lax.dynamic_slice_in_dim(padded_down, group_index * filters, filters, 0)
        tap_block = lax.dynamic_slice_in_dim(whole_weight, group_index * filters, filters, 1)
        section = conv_transpose(group_rows, tap_block, brick_shape)
        return running + lax.optimization_barrier(section.astype(jnp.bfloat16)).astype(jnp.float32)

    pool_grad = lax.fori_loop(
        0, count_filt, add_group, jnp.zeros((channels, brick_cells), jnp.float32)
    )
    hidden_grad = spread_cells(pool_grad.reshape((channels,) + brick_shape))
    first_down = (hidden_grad.reshape(channels, -1) * silu_slope(first_pre)).astype(jnp.bfloat16)
    first_grad = (
        lax.psum(conv_weights(first_down, padded_in, fine_shape), ("space", "filt")) * fine_scale
    )
    padded_back = pad_depth(
        extended(first_down.reshape((channels,) + fine_shape), (("space", 1), ("filt", 2)), 1)
    )
    volume_grad = (
        conv_transpose(padded_back, first_weight, fine_shape)
        .astype(jnp.bfloat16)
        .reshape((channels,) + fine_shape)
    )
    return (features, volume_grad, first_grad, second_grad)


def solution(mesh):
    placed = (
        P(None, "space", "filt", None),
        P(),
        P(None, "filt", None),
        P("filt", "space", None, None),
    )
    return jax.shard_map(
        local,
        mesh=mesh,
        in_specs=placed,
        out_specs=(
            P("filt", "space", None, None),
            P(None, "space", "filt", None),
            P(),
            P(None, "filt", None),
        ),
        check_vma=False,
    )
```

profile of v0, /device:TPU:0, one launch (start us, length us, event | category | flops | bytes accessed | tf_op | source)
XLA Modules:
  0.0 316.7 jit_solution(11860188222224926915)
XLA Ops:
  7.2 1.4 copy.107
  8.5 4.2 %all-to-all-start.1 = ((bf16[64,1,2,128]{3,0,1,2:T(8,128)(2,1)}), bf16[64,1,2,128]{3,0,1,2:T(8,128)(2,1)}, u32[]{:S(2)}, u32[]{:S(2)}) async-start(bf16[64,1,2,128]{3,0,1,2:T(8,128)(2,1)} %copy.107), calls=%async_computation.1 | async-start | bytes 65536 | tf_op jit(solution)/shard_map/all_to_all | solution.py:130
  15.0 3.0 collective-permute-start
  18.1 1.3 copy.96
  19.4 15.2 %all_gather.3 = bf16[27,128,64]{2,0,1:T(8,128)(2,1)S(1)} all-gather(bf16[27,64,64]{2,0,1:T(8,128)(2,1)S(1)} %copy.96), channel_id=1, replica_groups=mesh['space'=16,'filt'=2] {'filt'}, dimensions={1}, use_global_device_ids=true | all-gather | bytes 663552 | tf_op jit(solution)/shard_map/all_gather | solution.py:124
  37.6 4.2 %collective-permute-start.2 = (bf16[64,4,1,256]{3,2,1,0:T(2,128)(2,1)}, bf16[64,4,1,256]{3,2,1,0:T(2,128)(2,1)S(1)}, u32[]{:S(2)}, u32[]{:S(2)}) collective-permute-start(bf16[64,4,1,256]{3,2,1,0:T(2,128)(2,1)} %get-tuple-element.266), channel_id=1, source_target_pairs={{0,1},{2,3},{4,5},{6,7},{8,9},{10,11},{12,13},{14,15},{16,17},{18,... | collective-permute-start | bytes 393224 | tf_op jit(solution)/shard_map/ppermute | solution.py:15
  41.8 1.5 collective-permute-start.3
  45.5 1.8 copy.153
  48.3 1.6 copy.151
  50.0 1.6 copy.150
  51.6 1.6 copy.149
  56.1 1.4 rev.98
  70.2 1.7 pad_maximum_fusion.9
  75.6 2.4 select_maximum_fusion.2
  78.1 2.9 fusion.157
  94.4 3.0 collective-permute-start.4
  99.7 4.8 %collective-permute-start.6 = (bf16[64,3,1,128]{3,0,2,1:T(8,128)(2,1)S(1)}, bf16[64,3,1,128]{3,0,2,1:T(8,128)(2,1)S(1)}, u32[]{:S(2)}, u32[]{:S(2)}) collective-permute-start(bf16[64,3,1,128]{3,0,2,1:T(8,128)(2,1)S(1)} %pad_maximum_fusion.18), channel_id=1, source_target_pairs={{0,1},{2,3},{4,5},{6,7},{8,9},{10,11},{12,13},{14,15},{16,17},{18,... | collective-permute-start | bytes 147464 | tf_op jit(solution)/shard_map/ppermute | solution.py:15
  104.5 1.5 collective-permute-done.6
  109.5 3.3 %collective-permute-start.8 = (bf16[128,1,1,128]{0,3,2,1:T(8,128)(2,1)S(1)}, bf16[128,1,1,128]{0,3,2,1:T(8,128)(2,1)S(1)}, u32[]{:S(2)}, u32[]{:S(2)}) collective-permute-start(bf16[128,1,1,128]{0,3,2,1:T(8,128)(2,1)S(1)} %bitcast.409), channel_id=1, source_target_pairs={{0,2},{2,4},{4,6},{6,8},{8,10},{10,12},{12,14},{14,16},{16,18},{18... | collective-permute-start | bytes 98312 | tf_op jit(solution)/shard_map/ppermute | solution.py:15
  115.9 3.3 %all-to-all-start = ((bf16[2,2,4096]{2,1,0:T(2,128)(2,1)}), bf16[2,2,4096]{2,1,0:T(2,128)(2,1)S(1)}, u32[]{:S(2)}, u32[]{:S(2)}) async-start(bf16[2,2,4096]{2,1,0:T(2,128)(2,1)} %reshape.942), calls=%async_computation | async-start | bytes 65536 | tf_op jit(solution)/shard_map/all_to_all | solution.py:129
  130.1 4.6 %collective-permute-start.10 = (bf16[128,3,1,128]{0,3,2,1:T(8,128)(2,1)S(1)}, bf16[128,3,1,128]{0,3,2,1:T(8,128)(2,1)S(1)}, u32[]{:S(2)}, u32[]{:S(2)}) collective-permute-start(bf16[128,3,1,128]{0,3,2,1:T(8,128)(2,1)S(1)} %pad_maximum_fusion.17), channel_id=1, source_target_pairs={{0,1},{2,3},{4,5},{6,7},{8,9},{10,11},{12,13},{14,15},{16,17},{18,... | collective-permute-start | bytes 294920 | tf_op jit(solution)/shard_map/ppermute | solution.py:15
  137.4 5.5 %while.14 = (s32[]{:T(128)}, f32[64,128]{1,0:T(8,128)}, bf16[27,128,64]{2,1,0:T(8,128)(2,1)S(1)}, bf16[128,3,3,130]{3,0,2,1:T(8,128)(2,1)S(1)}, s32[]{:T(128)}, ...) while((s32[]{:T(128)}, f32[64,128]{1,0:T(8,128)}, ...), condition=%wide.region_2.3_spmd.clone, body=%wide.region_1.2_spmd.clone.sunk | while | flops 29736976 | bytes 3318213 | solution.py:149
  148.3 4.5 %collective-permute-start.12 = (bf16[64,1,2,256]{3,2,1,0:T(2,128)(2,1)S(1)}, bf16[64,1,2,256]{3,2,1,0:T(2,128)(2,1)S(1)}, u32[]{:S(2)}, u32[]{:S(2)}) collective-permute-start(bf16[64,1,2,256]{3,2,1,0:T(2,128)(2,1)S(1)} %get-tuple-element.272), channel_id=1, source_target_pairs={{0,2},{2,4},{4,6},{6,8},{8,10},{10,12},{12,14},{14,16},{16,18},{18... | collective-permute-start | bytes 196616 | tf_op jit(solution)/shard_map/ppermute | solution.py:15
  154.6 4.0 %collective-permute-start.14 = (bf16[64,4,1,256]{3,2,1,0:T(2,128)(2,1)S(1)}, bf16[64,4,1,256]{3,2,1,0:T(2,128)(2,1)S(1)}, u32[]{:S(2)}, u32[]{:S(2)}) collective-permute-start(bf16[64,4,1,256]{3,2,1,0:T(2,128)(2,1)S(1)} %get-tuple-element.261), channel_id=1, source_target_pairs={{0,1},{2,3},{4,5},{6,7},{8,9},{10,11},{12,13},{14,15},{16,17},{18,... | collective-permute-start | bytes 393224 | tf_op jit(solution)/shard_map/ppermute | solution.py:15
  158.6 1.6 collective-permute-start.15
  161.3 2.3 collective-permute-done.14
  163.6 4.7 %collective-permute-done.15 = bf16[64,4,1,256]{3,2,1,0:T(2,128)(2,1)S(1)} collective-permute-done((bf16[64,4,1,256]{3,2,1,0:T(2,128)(2,1)S(1)}, bf16[64,4,1,256]{3,2,1,0:T(2,128)(2,1)S(1)}, u32[]{:S(2)}, u32[]{:S(2)}) %collective-permute-start.15) | collective-permute-done | bytes 131104 | tf_op jit(solution)/shard_map/ppermute | solution.py:17
  168.3 1.7 pad_maximum_fusion.1
  172.4 2.4 select_maximum_fusion
  174.8 2.9 fusion.156
  186.0 120.2 %all-reduce.7.cloned.1.call-done = (f32[27,64,64]{1,2,0:T(8,128)}, f32[27,128,64]{2,1,0:T(8,128)}) async-done(((f32[27,64,64]{1,2,0:T(8,128)}, f32[27,128,64]{2,1,0:T(8,128)}), (f32[27,64,64]{1,2,0:T(8,128)}, f32[27,128,64]{2,1,0:T(8,128)})) %all-reduce.7.cloned.1.call-update) | async-done | bytes 1327120 | tf_op jit(solution)/shard_map/psum | solution.py:155
  306.2 1.4 broadcast_multiply_fusion
  (475 shorter events, 87.9 us)
Async XLA Ops:
  8.5 88.9 %all-to-all-start.1 = ((bf16[64,1,2,128]{3,0,1,2:T(8,128)(2,1)}), bf16[64,1,2,128]{3,0,1,2:T(8,128)(2,1)}, u32[]{:S(2)}, u32[]{:S(2)}) async-start(bf16[64,1,2,128]{3,0,1,2:T(8,128)(2,1)} %copy.107), calls=%async_computation.1 | async-start | bytes 65536 | tf_op jit(solution)/shard_map/all_to_all | solution.py:130
  13.7 22.2 %collective-permute-start.1 = (bf16[64,1,2,256]{3,2,1,0:T(2,128)(2,1)S(1)}, bf16[64,1,2,256]{3,2,1,0:T(2,128)(2,1)S(1)}, u32[]{:S(2)}, u32[]{:S(2)}) collective-permute-start(bf16[64,1,2,256]{3,2,1,0:T(2,128)(2,1)S(1)} %get-tuple-element.276), channel_id=1, source_target_pairs={{2,0},{4,2},{6,4},{8,6},{10,8},{12,10},{14,12},{16,14},{18,16},{20... | collective-permute-start | bytes 196616 | tf_op jit(solution)/shard_map/ppermute | solution.py:17
  15.0 20.9 %collective-permute-start = (bf16[64,1,2,256]{3,2,1,0:T(2,128)(2,1)S(1)}, bf16[64,1,2,256]{3,2,1,0:T(2,128)(2,1)S(1)}, u32[]{:S(2)}, u32[]{:S(2)}) collective-permute-start(bf16[64,1,2,256]{3,2,1,0:T(2,128)(2,1)S(1)} %get-tuple-element.277), channel_id=1, source_target_pairs={{0,2},{2,4},{4,6},{6,8},{8,10},{10,12},{12,14},{14,16},{16,18},{18... | collective-permute-start | bytes 196616 | tf_op jit(solution)/shard_map/ppermute | solution.py:15
  19.4 16.6 %copy-start.17 = (bf16[64,2,2,256]{3,2,1,0:T(2,128)(2,1)S(1)}, bf16[64,2,2,256]{3,2,1,0:T(2,128)(2,1)}, u32[]{:S(2)}) copy-start(bf16[64,2,2,256]{3,2,1,0:T(2,128)(2,1)} %param.6) | copy-start | bytes 393220
  37.6 32.6 %collective-permute-start.2 = (bf16[64,4,1,256]{3,2,1,0:T(2,128)(2,1)}, bf16[64,4,1,256]{3,2,1,0:T(2,128)(2,1)S(1)}, u32[]{:S(2)}, u32[]{:S(2)}) collective-permute-start(bf16[64,4,1,256]{3,2,1,0:T(2,128)(2,1)} %get-tuple-element.266), channel_id=1, source_target_pairs={{0,1},{2,3},{4,5},{6,7},{8,9},{10,11},{12,13},{14,15},{16,17},{18,... | collective-permute-start | bytes 393224 | tf_op jit(solution)/shard_map/ppermute | solution.py:15
  41.8 28.4 %collective-permute-start.3 = (bf16[64,4,1,256]{3,2,1,0:T(2,128)(2,1)}, bf16[64,4,1,256]{3,2,1,0:T(2,128)(2,1)S(1)}, u32[]{:S(2)}, u32[]{:S(2)}) collective-permute-start(bf16[64,4,1,256]{3,2,1,0:T(2,128)(2,1)} %get-tuple-element.267), channel_id=1, source_target_pairs={{1,0},{3,2},{5,4},{7,6},{9,8},{11,10},{13,12},{15,14},{17,16},{19,... | collective-permute-start | bytes 393224 | tf_op jit(solution)/shard_map/ppermute | solution.py:17
  45.4 15.7 %copy-start.62 = (bf16[64,3,64]{2,0,1:T(8,128)(2,1)S(1)}, bf16[64,3,64]{2,0,1:T(8,128)(2,1)}, u32[]{:S(2)}) copy-start(bf16[64,3,64]{2,0,1:T(8,128)(2,1)} %get-tuple-element.228) | copy-start | bytes 73732
  45.4 16.4 %copy-start.61 = (bf16[64,3,64]{2,0,1:T(8,128)(2,1)S(1)}, bf16[64,3,64]{2,0,1:T(8,128)(2,1)}, u32[]{:S(2)}) copy-start(bf16[64,3,64]{2,0,1:T(8,128)(2,1)} %get-tuple-element.229) | copy-start | bytes 73732
  45.4 17.1 %copy-start.60 = (bf16[64,3,64]{2,0,1:T(8,128)(2,1)S(1)}, bf16[64,3,64]{2,0,1:T(8,128)(2,1)}, u32[]{:S(2)}) copy-start(bf16[64,3,64]{2,0,1:T(8,128)(2,1)} %get-tuple-element.230) | copy-start | bytes 73732
  45.4 17.8 %copy-start.59 = (bf16[64,3,64]{2,0,1:T(8,128)(2,1)S(1)}, bf16[64,3,64]{2,0,1:T(8,128)(2,1)}, u32[]{:S(2)}) copy-start(bf16[64,3,64]{2,0,1:T(8,128)(2,1)} %get-tuple-element.231) | copy-start | bytes 73732
  45.5 18.5 %copy-start.58 = (bf16[3,64,64]{2,1,0:T(8,128)(2,1)S(1)}, bf16[3,64,64]{2,1,0:T(8,128)(2,1)}, u32[]{:S(2)}) copy-start(bf16[3,64,64]{2,1,0:T(8,128)(2,1)} %get-tuple-element.232) | copy-start | bytes 73732
  45.5 19.1 %copy-start.57 = (bf16[3,64,64]{2,1,0:T(8,128)(2,1)S(1)}, bf16[3,64,64]{2,1,0:T(8,128)(2,1)}, u32[]{:S(2)}) copy-start(bf16[3,64,64]{2,1,0:T(8,128)(2,1)} %get-tuple-element.233) | copy-start | bytes 73732
  45.5 19.7 %copy-start.56 = (bf16[3,64,64]{2,1,0:T(8,128)(2,1)S(1)}, bf16[3,64,64]{2,1,0:T(8,128)(2,1)}, u32[]{:S(2)}) copy-start(bf16[3,64,64]{2,1,0:T(8,128)(2,1)} %get-tuple-element.234) | copy-start | bytes 73732
  45.5 20.3 %copy-start.55 = (bf16[3,64,64]{2,1,0:T(8,128)(2,1)S(1)}, bf16[3,64,64]{2,1,0:T(8,128)(2,1)}, u32[]{:S(2)}) copy-start(bf16[3,64,64]{2,1,0:T(8,128)(2,1)} %get-tuple-element.235) | copy-start | bytes 73732
  45.5 20.9 %copy-start.54 = (bf16[3,64,64]{2,1,0:T(8,128)(2,1)S(1)}, bf16[3,64,64]{2,1,0:T(8,128)(2,1)}, u32[]{:S(2)}) copy-start(bf16[3,64,64]{2,1,0:T(8,128)(2,1)} %get-tuple-element.236) | copy-start | bytes 73732
  45.5 21.5 %copy-start.53 = (bf16[3,64,64]{2,1,0:T(8,128)(2,1)S(1)}, bf16[3,64,64]{2,1,0:T(8,128)(2,1)}, u32[]{:S(2)}) copy-start(bf16[3,64,64]{2,1,0:T(8,128)(2,1)} %get-tuple-element.237) | copy-start | bytes 73732
  45.5 22.1 %copy-start.52 = (bf16[3,64,64]{2,1,0:T(8,128)(2,1)S(1)}, bf16[3,64,64]{2,1,0:T(8,128)(2,1)}, u32[]{:S(2)}) copy-start(bf16[3,64,64]{2,1,0:T(8,128)(2,1)} %get-tuple-element.238) | copy-start | bytes 73732
  45.5 22.8 %copy-start.51 = (bf16[3,64,64]{2,1,0:T(8,128)(2,1)S(1)}, bf16[3,64,64]{2,1,0:T(8,128)(2,1)}, u32[]{:S(2)}) copy-start(bf16[3,64,64]{2,1,0:T(8,128)(2,1)} %get-tuple-element.239) | copy-start | bytes 73732
  93.1 5.2 %collective-permute-start.5 = (bf16[64,1,1,128]{3,0,2,1:T(8,128)(2,1)S(1)}, bf16[64,1,1,128]{3,0,2,1:T(8,128)(2,1)S(1)}, u32[]{:S(2)}, u32[]{:S(2)}) collective-permute-start(bf16[64,1,1,128]{3,0,2,1:T(8,128)(2,1)S(1)} %fusion.245), channel_id=1, source_target_pairs={{2,0},{4,2},{6,4},{8,6},{10,8},{12,10},{14,12},{16,14},{18,16},{20... | collective-permute-start | bytes 49160 | tf_op jit(solution)/shard_map/ppermute | solution.py:17
  94.4 3.9 %collective-permute-start.4 = (bf16[64,1,1,128]{3,0,2,1:T(8,128)(2,1)S(1)}, bf16[64,1,1,128]{3,0,2,1:T(8,128)(2,1)S(1)}, u32[]{:S(2)}, u32[]{:S(2)}) collective-permute-start(bf16[64,1,1,128]{3,0,2,1:T(8,128)(2,1)S(1)} %fusion.245), channel_id=1, source_target_pairs={{0,2},{2,4},{4,6},{6,8},{8,10},{10,12},{12,14},{14,16},{16,18},{18... | collective-permute-start | bytes 49160 | tf_op jit(solution)/shard_map/ppermute | solution.py:15
  98.4 6.1 %collective-permute-start.7 = (bf16[64,3,1,128]{3,0,2,1:T(8,128)(2,1)S(1)}, bf16[64,3,1,128]{3,0,2,1:T(8,128)(2,1)S(1)}, u32[]{:S(2)}, u32[]{:S(2)}) collective-permute-start(bf16[64,3,1,128]{3,0,2,1:T(8,128)(2,1)S(1)} %pad_maximum_fusion.18), channel_id=1, source_target_pairs={{1,0},{3,2},{5,4},{7,6},{9,8},{11,10},{13,12},{15,14},{17,16},{19,... | collective-permute-start | bytes 147464 | tf_op jit(solution)/shard_map/ppermute | solution.py:17
  99.7 6.3 %collective-permute-start.6 = (bf16[64,3,1,128]{3,0,2,1:T(8,128)(2,1)S(1)}, bf16[64,3,1,128]{3,0,2,1:T(8,128)(2,1)S(1)}, u32[]{:S(2)}, u32[]{:S(2)}) collective-permute-start(bf16[64,3,1,128]{3,0,2,1:T(8,128)(2,1)S(1)} %pad_maximum_fusion.18), channel_id=1, source_target_pairs={{0,1},{2,3},{4,5},{6,7},{8,9},{10,11},{12,13},{14,15},{16,17},{18,... | collective-permute-start | bytes 147464 | tf_op jit(solution)/shard_map/ppermute | solution.py:15
  108.2 20.6 %collective-permute-start.9 = (bf16[128,1,1,128]{0,3,2,1:T(8,128)(2,1)S(1)}, bf16[128,1,1,128]{0,3,2,1:T(8,128)(2,1)S(1)}, u32[]{:S(2)}, u32[]{:S(2)}) collective-permute-start(bf16[128,1,1,128]{0,3,2,1:T(8,128)(2,1)S(1)} %bitcast.408), channel_id=1, source_target_pairs={{2,0},{4,2},{6,4},{8,6},{10,8},{12,10},{14,12},{16,14},{18,16},{20... | collective-permute-start | bytes 98312 | tf_op jit(solution)/shard_map/ppermute | solution.py:17
  109.5 19.3 %collective-permute-start.8 = (bf16[128,1,1,128]{0,3,2,1:T(8,128)(2,1)S(1)}, bf16[128,1,1,128]{0,3,2,1:T(8,128)(2,1)S(1)}, u32[]{:S(2)}, u32[]{:S(2)}) collective-permute-start(bf16[128,1,1,128]{0,3,2,1:T(8,128)(2,1)S(1)} %bitcast.409), channel_id=1, source_target_pairs={{0,2},{2,4},{4,6},{6,8},{8,10},{10,12},{12,14},{14,16},{16,18},{18... | collective-permute-start | bytes 98312 | tf_op jit(solution)/shard_map/ppermute | solution.py:15
  115.9 18.9 %all-to-all-start = ((bf16[2,2,4096]{2,1,0:T(2,128)(2,1)}), bf16[2,2,4096]{2,1,0:T(2,128)(2,1)S(1)}, u32[]{:S(2)}, u32[]{:S(2)}) async-start(bf16[2,2,4096]{2,1,0:T(2,128)(2,1)} %reshape.942), calls=%async_computation | async-start | bytes 65536 | tf_op jit(solution)/shard_map/all_to_all | solution.py:129
  119.2 187.0 %all-reduce.7.cloned.1.call-start = ((), (), s32[]{:S(2)}) async-start(), calls=%async_computation.2 | async-start | bytes 5308416 | tf_op jit(solution)/shard_map/psum | solution.py:155
  128.8 6.7 %collective-permute-start.11 = (bf16[128,3,1,128]{0,3,2,1:T(8,128)(2,1)S(1)}, bf16[128,3,1,128]{0,3,2,1:T(8,128)(2,1)S(1)}, u32[]{:S(2)}, u32[]{:S(2)}) collective-permute-start(bf16[128,3,1,128]{0,3,2,1:T(8,128)(2,1)S(1)} %pad_maximum_fusion.17), channel_id=1, source_target_pairs={{1,0},{3,2},{5,4},{7,6},{9,8},{11,10},{13,12},{15,14},{17,16},{19,... | collective-permute-start | bytes 294920 | tf_op jit(solution)/shard_map/ppermute | solution.py:17
  130.1 6.8 %collective-permute-start.10 = (bf16[128,3,1,128]{0,3,2,1:T(8,128)(2,1)S(1)}, bf16[128,3,1,128]{0,3,2,1:T(8,128)(2,1)S(1)}, u32[]{:S(2)}, u32[]{:S(2)}) collective-permute-start(bf16[128,3,1,128]{0,3,2,1:T(8,128)(2,1)S(1)} %pad_maximum_fusion.17), channel_id=1, source_target_pairs={{0,1},{2,3},{4,5},{6,7},{8,9},{10,11},{12,13},{14,15},{16,17},{18,... | collective-permute-start | bytes 294920 | tf_op jit(solution)/shard_map/ppermute | solution.py:15
  147.0 6.7 %collective-permute-start.13 = (bf16[64,1,2,256]{3,2,1,0:T(2,128)(2,1)S(1)}, bf16[64,1,2,256]{3,2,1,0:T(2,128)(2,1)S(1)}, u32[]{:S(2)}, u32[]{:S(2)}) collective-permute-start(bf16[64,1,2,256]{3,2,1,0:T(2,128)(2,1)S(1)} %get-tuple-element.271), channel_id=1, source_target_pairs={{2,0},{4,2},{6,4},{8,6},{10,8},{12,10},{14,12},{16,14},{18,16},{20... | collective-permute-start | bytes 196616 | tf_op jit(solution)/shard_map/ppermute | solution.py:17
  148.3 5.4 %collective-permute-start.12 = (bf16[64,1,2,256]{3,2,1,0:T(2,128)(2,1)S(1)}, bf16[64,1,2,256]{3,2,1,0:T(2,128)(2,1)S(1)}, u32[]{:S(2)}, u32[]{:S(2)}) collective-permute-start(bf16[64,1,2,256]{3,2,1,0:T(2,128)(2,1)S(1)} %get-tuple-element.272), channel_id=1, source_target_pairs={{0,2},{2,4},{4,6},{6,8},{8,10},{10,12},{12,14},{14,16},{16,18},{18... | collective-permute-start | bytes 196616 | tf_op jit(solution)/shard_map/ppermute | solution.py:15
  154.6 9.0 %collective-permute-start.14 = (bf16[64,4,1,256]{3,2,1,0:T(2,128)(2,1)S(1)}, bf16[64,4,1,256]{3,2,1,0:T(2,128)(2,1)S(1)}, u32[]{:S(2)}, u32[]{:S(2)}) collective-permute-start(bf16[64,4,1,256]{3,2,1,0:T(2,128)(2,1)S(1)} %get-tuple-element.261), channel_id=1, source_target_pairs={{0,1},{2,3},{4,5},{6,7},{8,9},{10,11},{12,13},{14,15},{16,17},{18,... | collective-permute-start | bytes 393224 | tf_op jit(solution)/shard_map/ppermute | solution.py:15
  158.6 9.7 %collective-permute-start.15 = (bf16[64,4,1,256]{3,2,1,0:T(2,128)(2,1)S(1)}, bf16[64,4,1,256]{3,2,1,0:T(2,128)(2,1)S(1)}, u32[]{:S(2)}, u32[]{:S(2)}) collective-permute-start(bf16[64,4,1,256]{3,2,1,0:T(2,128)(2,1)S(1)} %get-tuple-element.262), channel_id=1, source_target_pairs={{1,0},{3,2},{5,4},{7,6},{9,8},{11,10},{13,12},{15,14},{17,16},{19,... | collective-permute-start | bytes 393224 | tf_op jit(solution)/shard_map/ppermute | solution.py:17
  (82 other events, 338.1 us)
Sparse Core Ops, SparseCore 0:
  161.2 144.9 all-reduce.6
where the time goes:
time: 318 us; the launch traced here: 317 us
  waiting for transfers between devices  131 us (41%)
  local copies, waits for them, and re-layouts  75.2 us (24%)
  starting transfers between devices  49.8 us (16%)
  between operations  16.3 us (5%)
  blocking collectives  15.2 us (5%)
  matrix products  14.6 us (5%)
  other arithmetic  14.5 us (5%)
    psum x1, waiting for transfers between devices, local(): lax.psum(conv_weights(first_down, padded_in, fine_shape), ('space', 'filt'))  120 us
    ppermute x8, starting transfers between devices, extended(): lax.ppermute(tail, axis, [(i, (i + 1) % count) for i in range(ends)])  31.4 us
    unnamed x237, local copies, waits for them, and re-layouts  25.8 us
    reshape x58, local copies, waits for them, and re-layouts, window(): return section.reshape(padded.shape[0], extent_x * extent_y * extent_z)  17.6 us
    all_gather x1, blocking collectives, local(): whole_weight = lax.all_gather(second_weight, 'filt', axis=1, tiled=True)  15.2 us
    ppermute x8, starting transfers between devices, extended(): lax.ppermute(head, axis, [((i + 1) % count, i) for i in range(ends)])  10.8 us
    concatenate x10, other arithmetic, extended(): jnp.concatenate([lax.ppermute(tail, axis, [(i, (i + 1) % count) for i in...  9.21 us
    rev x27, local copies, waits for them, and re-layouts, conv_transpose(): tap_block = weight[24 - tap_base:27 - tap_base][::-1]  6.46 us
  transfers between devices with their start and end apart: 19, of which 6 were waited for; matrix products, arithmetic and copies ran while one was open for 27% of the time, Pallas kernels for 0%

commit v1 on v0

--- a/solution.py
+++ b/solution.py
@@ -151,9 +151,8 @@
     )
     hidden_grad = spread_cells(pool_grad.reshape((channels,) + brick_shape))
     first_down = (hidden_grad.reshape(channels, -1) * silu_slope(first_pre)).astype(jnp.bfloat16)
-    first_grad = (
-        lax.psum(conv_weights(first_down, padded_in, fine_shape), ("space", "filt")) * fine_scale
-    )
+    _pair_body = lambda s0: lax.psum(lax.psum(s0, "space"), "filt")
+    first_grad = _pair_body(conv_weights(first_down, padded_in, fine_shape)) * fine_scale
     padded_back = pad_depth(
         extended(first_down.reshape((channels,) + fine_shape), (("space", 1), ("filt", 2)), 1)
     )

time: 318 us -> 450 us (1.42)
  waiting for transfers between devices: 131 us -> 252 us
    psum x1 -> x3, waiting for transfers between devices: 120 us -> 243 us  [the longest x1 136 us: local(): lax.psum(conv_weights(down_grad, padded_pool, brick_shape), ('space', 'fi...]
    unnamed x237 -> x219, local copies, waits for them, and re-layouts: 25.8 us -> 24.7 us
  transfers between devices with their start and end apart: 19 -> 21, of which waited for: 6 -> 7; matrix products, arithmetic and copies ran while one was open for 27% -> 23% of each run, Pallas kernels for 0% -> 0%
where the time goes in v1:
time: 450 us; the launch traced here: 448 us
  waiting for transfers between devices  252 us (56%)
  local copies, waits for them, and re-layouts  77.8 us (17%)
  starting transfers between devices  50.5 us (11%)
  other arithmetic  18.1 us (4%)
  matrix products  18.1 us (4%)
  between operations  16 us (4%)
  blocking collectives  15.2 us (3%)
    psum x1, waiting for transfers between devices, local(): lax.psum(conv_weights(down_grad, padded_pool, brick_shape), ('space', 'fi...  136 us
    psum x2, waiting for transfers between devices, local(): _pair_body = lambda s0: lax.psum(lax.psum(s0, 'space'), 'filt')  107 us
    ppermute x8, starting transfers between devices, extended(): lax.ppermute(tail, axis, [(i, (i + 1) % count) for i in range(ends)])  31.5 us
    unnamed x219, local copies, waits for them, and re-layouts  24.7 us
    reshape x58, local copies, waits for them, and re-layouts, window(): return section.reshape(padded.shape[0], extent_x * extent_y * extent_z)  17.6 us
    all_gather x1, blocking collectives, local(): whole_weight = lax.all_gather(second_weight, 'filt', axis=1, tiled=True)  15.2 us
    concatenate x10, other arithmetic, extended(): jnp.concatenate([lax.ppermute(tail, axis, [(i, (i + 1) % count) for i in...  10.7 us
    ppermute x8, starting transfers between devices, extended(): lax.ppermute(head, axis, [((i + 1) % count, i) for i in range(ends)])  10.5 us
  transfers between devices with their start and end apart: 21, of which 7 were waited for; matrix products, arithmetic and copies ran while one was open for 23% of the time, Pallas kernels for 0%

profile of v1, /device:TPU:0, one launch (start us, length us, event | category | flops | bytes accessed | tf_op | source)
XLA Modules:
  0.0 447.9 jit_solution(2193131205420616696)
XLA Ops:
  8.5 4.2 all-to-all-start.1
  15.0 3.0 collective-permute-start
  19.4 15.2 %all_gather.3 = bf16[27,128,64]{2,0,1:T(8,128)(2,1)S(1)} all-gather(bf16[27,64,64]{2,0,1:T(8,128)(2,1)S(1)} %copy.96), channel_id=1, replica_groups=mesh['space'=16,'filt'=2] {'filt'}, dimensions={1}, use_global_device_ids=true | all-gather | bytes 663552 | tf_op jit(solution)/shard_map/all_gather | solution.py:124
  37.6 4.2 collective-permute-start.2
  45.5 1.8 copy.153
  48.3 1.6 copy.151
  50.0 1.6 copy.150
  51.6 1.6 copy.149
  70.3 1.7 pad_maximum_fusion.9
  75.7 2.4 select_maximum_fusion.2
  78.1 2.9 fusion.157
  98.0 3.0 collective-permute-start.4
  103.3 4.8 %collective-permute-start.6 = (bf16[64,3,1,128]{3,0,2,1:T(8,128)(2,1)S(1)}, bf16[64,3,1,128]{3,0,2,1:T(8,128)(2,1)S(1)}, u32[]{:S(2)}, u32[]{:S(2)}) collective-permute-start(bf16[64,3,1,128]{3,0,2,1:T(8,128)(2,1)S(1)} %pad_maximum_fusion.18), channel_id=1, source_target_pairs={{0,1},{2,3},{4,5},{6,7},{8,9},{10,11},{12,13},{14,15},{16,17},{18,... | collective-permute-start | bytes 147464 | tf_op jit(solution)/shard_map/ppermute | solution.py:15
  108.1 1.5 collective-permute-done.6
  113.1 3.9 collective-permute-start.8
  122.6 3.9 all-to-all-start
  128.1 1.7 copy.125
  129.8 1.7 copy.124
  131.5 1.7 copy.123
  139.5 4.6 %collective-permute-start.10 = (bf16[128,3,1,128]{0,3,2,1:T(8,128)(2,1)S(1)}, bf16[128,3,1,128]{0,3,2,1:T(8,128)(2,1)S(1)}, u32[]{:S(2)}, u32[]{:S(2)}) collective-permute-start(bf16[128,3,1,128]{0,3,2,1:T(8,128)(2,1)S(1)} %pad_maximum_fusion.17), channel_id=1, source_target_pairs={{0,1},{2,3},{4,5},{6,7},{8,9},{10,11},{12,13},{14,15},{16,17},{18,... | collective-permute-start | bytes 294920 | tf_op jit(solution)/shard_map/ppermute | solution.py:15
  147.5 5.5 %while.14 = (s32[]{:T(128)}, f32[64,128]{1,0:T(8,128)}, bf16[27,128,64]{2,1,0:T(8,128)(2,1)S(1)}, bf16[128,3,3,130]{3,0,2,1:T(8,128)(2,1)S(1)}, s32[]{:T(128)}, ...) while((s32[]{:T(128)}, f32[64,128]{1,0:T(8,128)}, ...), condition=%wide.region_2.3_spmd.clone, body=%wide.region_1.2_spmd.clone.sunk | while | flops 29736976 | bytes 3318213 | solution.py:149
  159.2 3.9 collective-permute-start.12
  165.2 4.0 collective-permute-start.14
  173.2 1.6 collective-permute-done.14
  174.8 4.7 %collective-permute-done.15 = bf16[64,4,1,256]{3,2,1,0:T(2,128)(2,1)S(1)} collective-permute-done((bf16[64,4,1,256]{3,2,1,0:T(2,128)(2,1)S(1)}, bf16[64,4,1,256]{3,2,1,0:T(2,128)(2,1)S(1)}, u32[]{:S(2)}, u32[]{:S(2)}) %collective-permute-start.15) | collective-permute-done | bytes 131104 | tf_op jit(solution)/shard_map/ppermute | solution.py:17
  179.5 1.7 pad_maximum_fusion.1
  182.9 2.4 select_maximum_fusion
  185.3 2.9 fusion.156
  192.3 70.8 %all-reduce.8.cloned.1.call-done = f32[27,64,64]{1,2,0:T(8,128)} async-done(((f32[27,64,64]{1,2,0:T(8,128)}), f32[27,64,64]{1,2,0:T(8,128)}) %all-reduce.8.cloned.1.call-update) | async-done | bytes 442384 | tf_op jit(solution)/shard_map/psum | solution.py:154
  264.6 135.7 %all-reduce.12.cloned.1.call-done = f32[27,128,64]{2,1,0:T(8,128)} async-done(((f32[27,128,64]{2,1,0:T(8,128)}), f32[27,128,64]{2,1,0:T(8,128)}) %all-reduce.12.cloned.1.call-update) | async-done | bytes 884752 | tf_op jit(solution)/shard_map/psum | solution.py:134
  400.3 2.2 dynamic-slice_multiply_fusion
  402.4 36.4 %all-reduce.10.cloned.1.call-done = f32[27,64,64]{1,2,0:T(8,128)} async-done(((f32[27,64,64]{1,2,0:T(8,128)}), f32[27,64,64]{1,2,0:T(8,128)}) %all-reduce.10.cloned.1.call-update) | async-done | bytes 442384 | tf_op jit(solution)/shard_map/psum | solution.py:154
  (463 shorter events, 98.2 us)
Async XLA Ops:
  8.5 92.5 %all-to-all-start.1 = ((bf16[64,1,2,128]{3,0,1,2:T(8,128)(2,1)}), bf16[64,1,2,128]{3,0,1,2:T(8,128)(2,1)}, u32[]{:S(2)}, u32[]{:S(2)}) async-start(bf16[64,1,2,128]{3,0,1,2:T(8,128)(2,1)} %copy.107), calls=%async_computation.1 | async-start | bytes 65536 | tf_op jit(solution)/shard_map/all_to_all | solution.py:130
  13.7 22.2 %collective-permute-start.1 = (bf16[64,1,2,256]{3,2,1,0:T(2,128)(2,1)S(1)}, bf16[64,1,2,256]{3,2,1,0:T(2,128)(2,1)S(1)}, u32[]{:S(2)}, u32[]{:S(2)}) collective-permute-start(bf16[64,1,2,256]{3,2,1,0:T(2,128)(2,1)S(1)} %get-tuple-element.274), channel_id=1, source_target_pairs={{2,0},{4,2},{6,4},{8,6},{10,8},{12,10},{14,12},{16,14},{18,16},{20... | collective-permute-start | bytes 196616 | tf_op jit(solution)/shard_map/ppermute | solution.py:17
  15.0 20.9 %collective-permute-start = (bf16[64,1,2,256]{3,2,1,0:T(2,128)(2,1)S(1)}, bf16[64,1,2,256]{3,2,1,0:T(2,128)(2,1)S(1)}, u32[]{:S(2)}, u32[]{:S(2)}) collective-permute-start(bf16[64,1,2,256]{3,2,1,0:T(2,128)(2,1)S(1)} %get-tuple-element.275), channel_id=1, source_target_pairs={{0,2},{2,4},{4,6},{6,8},{8,10},{10,12},{12,14},{14,16},{16,18},{18... | collective-permute-start | bytes 196616 | tf_op jit(solution)/shard_map/ppermute | solution.py:15
  37.6 32.7 %collective-permute-start.2 = (bf16[64,4,1,256]{3,2,1,0:T(2,128)(2,1)}, bf16[64,4,1,256]{3,2,1,0:T(2,128)(2,1)S(1)}, u32[]{:S(2)}, u32[]{:S(2)}) collective-permute-start(bf16[64,4,1,256]{3,2,1,0:T(2,128)(2,1)} %get-tuple-element.264), channel_id=1, source_target_pairs={{0,1},{2,3},{4,5},{6,7},{8,9},{10,11},{12,13},{14,15},{16,17},{18,... | collective-permute-start | bytes 393224 | tf_op jit(solution)/shard_map/ppermute | solution.py:15
  41.8 28.5 %collective-permute-start.3 = (bf16[64,4,1,256]{3,2,1,0:T(2,128)(2,1)}, bf16[64,4,1,256]{3,2,1,0:T(2,128)(2,1)S(1)}, u32[]{:S(2)}, u32[]{:S(2)}) collective-permute-start(bf16[64,4,1,256]{3,2,1,0:T(2,128)(2,1)} %get-tuple-element.265), channel_id=1, source_target_pairs={{1,0},{3,2},{5,4},{7,6},{9,8},{11,10},{13,12},{15,14},{17,16},{19,... | collective-permute-start | bytes 393224 | tf_op jit(solution)/shard_map/ppermute | solution.py:17
  45.4 17.8 %copy-start.55 = (bf16[64,3,64]{2,0,1:T(8,128)(2,1)S(1)}, bf16[64,3,64]{2,0,1:T(8,128)(2,1)}, u32[]{:S(2)}) copy-start(bf16[64,3,64]{2,0,1:T(8,128)(2,1)} %get-tuple-element.229) | copy-start | bytes 73732
  45.4 18.5 %copy-start.54 = (bf16[3,64,64]{2,1,0:T(8,128)(2,1)S(1)}, bf16[3,64,64]{2,1,0:T(8,128)(2,1)}, u32[]{:S(2)}) copy-start(bf16[3,64,64]{2,1,0:T(8,128)(2,1)} %get-tuple-element.230) | copy-start | bytes 73732
  45.5 19.1 %copy-start.53 = (bf16[3,64,64]{2,1,0:T(8,128)(2,1)S(1)}, bf16[3,64,64]{2,1,0:T(8,128)(2,1)}, u32[]{:S(2)}) copy-start(bf16[3,64,64]{2,1,0:T(8,128)(2,1)} %get-tuple-element.231) | copy-start | bytes 73732
  45.5 19.7 %copy-start.52 = (bf16[3,64,64]{2,1,0:T(8,128)(2,1)S(1)}, bf16[3,64,64]{2,1,0:T(8,128)(2,1)}, u32[]{:S(2)}) copy-start(bf16[3,64,64]{2,1,0:T(8,128)(2,1)} %get-tuple-element.232) | copy-start | bytes 73732
  45.5 20.3 %copy-start.51 = (bf16[3,64,64]{2,1,0:T(8,128)(2,1)S(1)}, bf16[3,64,64]{2,1,0:T(8,128)(2,1)}, u32[]{:S(2)}) copy-start(bf16[3,64,64]{2,1,0:T(8,128)(2,1)} %get-tuple-element.233) | copy-start | bytes 73732
  45.5 20.9 %copy-start.50 = (bf16[3,64,64]{2,1,0:T(8,128)(2,1)S(1)}, bf16[3,64,64]{2,1,0:T(8,128)(2,1)}, u32[]{:S(2)}) copy-start(bf16[3,64,64]{2,1,0:T(8,128)(2,1)} %get-tuple-element.234) | copy-start | bytes 73732
  45.5 21.5 %copy-start.49 = (bf16[3,64,64]{2,1,0:T(8,128)(2,1)S(1)}, bf16[3,64,64]{2,1,0:T(8,128)(2,1)}, u32[]{:S(2)}) copy-start(bf16[3,64,64]{2,1,0:T(8,128)(2,1)} %get-tuple-element.235) | copy-start | bytes 73732
  45.5 22.2 %copy-start.48 = (bf16[3,64,64]{2,1,0:T(8,128)(2,1)S(1)}, bf16[3,64,64]{2,1,0:T(8,128)(2,1)}, u32[]{:S(2)}) copy-start(bf16[3,64,64]{2,1,0:T(8,128)(2,1)} %get-tuple-element.236) | copy-start | bytes 73732
  45.5 22.8 %copy-start.47 = (bf16[3,64,64]{2,1,0:T(8,128)(2,1)S(1)}, bf16[3,64,64]{2,1,0:T(8,128)(2,1)}, u32[]{:S(2)}) copy-start(bf16[3,64,64]{2,1,0:T(8,128)(2,1)} %get-tuple-element.237) | copy-start | bytes 73732
  96.7 5.2 %collective-permute-start.5 = (bf16[64,1,1,128]{3,0,2,1:T(8,128)(2,1)S(1)}, bf16[64,1,1,128]{3,0,2,1:T(8,128)(2,1)S(1)}, u32[]{:S(2)}, u32[]{:S(2)}) collective-permute-start(bf16[64,1,1,128]{3,0,2,1:T(8,128)(2,1)S(1)} %fusion.245), channel_id=1, source_target_pairs={{2,0},{4,2},{6,4},{8,6},{10,8},{12,10},{14,12},{16,14},{18,16},{20... | collective-permute-start | bytes 49160 | tf_op jit(solution)/shard_map/ppermute | solution.py:17
  98.0 3.9 collective-permute-start.4
  102.0 6.1 %collective-permute-start.7 = (bf16[64,3,1,128]{3,0,2,1:T(8,128)(2,1)S(1)}, bf16[64,3,1,128]{3,0,2,1:T(8,128)(2,1)S(1)}, u32[]{:S(2)}, u32[]{:S(2)}) collective-permute-start(bf16[64,3,1,128]{3,0,2,1:T(8,128)(2,1)S(1)} %pad_maximum_fusion.18), channel_id=1, source_target_pairs={{1,0},{3,2},{5,4},{7,6},{9,8},{11,10},{13,12},{15,14},{17,16},{19,... | collective-permute-start | bytes 147464 | tf_op jit(solution)/shard_map/ppermute | solution.py:17
  103.3 6.3 %collective-permute-start.6 = (bf16[64,3,1,128]{3,0,2,1:T(8,128)(2,1)S(1)}, bf16[64,3,1,128]{3,0,2,1:T(8,128)(2,1)S(1)}, u32[]{:S(2)}, u32[]{:S(2)}) collective-permute-start(bf16[64,3,1,128]{3,0,2,1:T(8,128)(2,1)S(1)} %pad_maximum_fusion.18), channel_id=1, source_target_pairs={{0,1},{2,3},{4,5},{6,7},{8,9},{10,11},{12,13},{14,15},{16,17},{18,... | collective-permute-start | bytes 147464 | tf_op jit(solution)/shard_map/ppermute | solution.py:15
  111.8 24.5 %collective-permute-start.9 = (bf16[128,1,1,128]{0,3,2,1:T(8,128)(2,1)S(1)}, bf16[128,1,1,128]{0,3,2,1:T(8,128)(2,1)S(1)}, u32[]{:S(2)}, u32[]{:S(2)}) collective-permute-start(bf16[128,1,1,128]{0,3,2,1:T(8,128)(2,1)S(1)} %bitcast.408), channel_id=1, source_target_pairs={{2,0},{4,2},{6,4},{8,6},{10,8},{12,10},{14,12},{16,14},{18,16},{20... | collective-permute-start | bytes 98312 | tf_op jit(solution)/shard_map/ppermute | solution.py:17
  113.1 23.2 %collective-permute-start.8 = (bf16[128,1,1,128]{0,3,2,1:T(8,128)(2,1)S(1)}, bf16[128,1,1,128]{0,3,2,1:T(8,128)(2,1)}, u32[]{:S(2)}, u32[]{:S(2)}) collective-permute-start(bf16[128,1,1,128]{0,3,2,1:T(8,128)(2,1)S(1)} %bitcast.409), channel_id=1, source_target_pairs={{0,2},{2,4},{4,6},{6,8},{8,10},{10,12},{12,14},{14,16},{16,18},{18... | collective-permute-start | bytes 98312 | tf_op jit(solution)/shard_map/ppermute | solution.py:15
  122.6 48.9 %all-to-all-start = ((bf16[2,2,4096]{2,1,0:T(2,128)(2,1)}), bf16[2,2,4096]{2,1,0:T(2,128)(2,1)}, u32[]{:S(2)}, u32[]{:S(2)}) async-start(bf16[2,2,4096]{2,1,0:T(2,128)(2,1)} %reshape.942), calls=%async_computation | async-start | bytes 65536 | tf_op jit(solution)/shard_map/all_to_all | solution.py:129
  126.5 136.6 %all-reduce.8.cloned.1.call-start = ((), (), s32[]{:S(2)}) async-start(), calls=%async_computation.2 | async-start | bytes 1769472 | tf_op jit(solution)/shard_map/psum | solution.py:154
  138.2 6.9 %collective-permute-start.11 = (bf16[128,3,1,128]{0,3,2,1:T(8,128)(2,1)S(1)}, bf16[128,3,1,128]{0,3,2,1:T(8,128)(2,1)S(1)}, u32[]{:S(2)}, u32[]{:S(2)}) collective-permute-start(bf16[128,3,1,128]{0,3,2,1:T(8,128)(2,1)S(1)} %pad_maximum_fusion.17), channel_id=1, source_target_pairs={{1,0},{3,2},{5,4},{7,6},{9,8},{11,10},{13,12},{15,14},{17,16},{19,... | collective-permute-start | bytes 294920 | tf_op jit(solution)/shard_map/ppermute | solution.py:17
  139.5 6.8 %collective-permute-start.10 = (bf16[128,3,1,128]{0,3,2,1:T(8,128)(2,1)S(1)}, bf16[128,3,1,128]{0,3,2,1:T(8,128)(2,1)S(1)}, u32[]{:S(2)}, u32[]{:S(2)}) collective-permute-start(bf16[128,3,1,128]{0,3,2,1:T(8,128)(2,1)S(1)} %pad_maximum_fusion.17), channel_id=1, source_target_pairs={{0,1},{2,3},{4,5},{6,7},{8,9},{10,11},{12,13},{14,15},{16,17},{18,... | collective-permute-start | bytes 294920 | tf_op jit(solution)/shard_map/ppermute | solution.py:15
  157.9 6.4 %collective-permute-start.13 = (bf16[64,1,2,256]{3,2,1,0:T(2,128)(2,1)S(1)}, bf16[64,1,2,256]{3,2,1,0:T(2,128)(2,1)S(1)}, u32[]{:S(2)}, u32[]{:S(2)}) collective-permute-start(bf16[64,1,2,256]{3,2,1,0:T(2,128)(2,1)S(1)} %get-tuple-element.269), channel_id=1, source_target_pairs={{2,0},{4,2},{6,4},{8,6},{10,8},{12,10},{14,12},{16,14},{18,16},{20... | collective-permute-start | bytes 196616 | tf_op jit(solution)/shard_map/ppermute | solution.py:17
  159.2 5.1 %collective-permute-start.12 = (bf16[64,1,2,256]{3,2,1,0:T(2,128)(2,1)S(1)}, bf16[64,1,2,256]{3,2,1,0:T(2,128)(2,1)S(1)}, u32[]{:S(2)}, u32[]{:S(2)}) collective-permute-start(bf16[64,1,2,256]{3,2,1,0:T(2,128)(2,1)S(1)} %get-tuple-element.270), channel_id=1, source_target_pairs={{0,2},{2,4},{4,6},{6,8},{8,10},{10,12},{12,14},{14,16},{16,18},{18... | collective-permute-start | bytes 196616 | tf_op jit(solution)/shard_map/ppermute | solution.py:15
  164.2 236.0 %all-reduce.12.cloned.1.call-start = ((), (), s32[]{:S(2)}) async-start(), calls=%async_computation.4 | async-start | bytes 3538944 | tf_op jit(solution)/shard_map/psum | solution.py:134
  165.2 9.6 %collective-permute-start.14 = (bf16[64,4,1,256]{3,2,1,0:T(2,128)(2,1)S(1)}, bf16[64,4,1,256]{3,2,1,0:T(2,128)(2,1)S(1)}, u32[]{:S(2)}, u32[]{:S(2)}) collective-permute-start(bf16[64,4,1,256]{3,2,1,0:T(2,128)(2,1)S(1)} %get-tuple-element.259), channel_id=1, source_target_pairs={{0,1},{2,3},{4,5},{6,7},{8,9},{10,11},{12,13},{14,15},{16,17},{18,... | collective-permute-start | bytes 393224 | tf_op jit(solution)/shard_map/ppermute | solution.py:15
  169.2 10.3 %collective-permute-start.15 = (bf16[64,4,1,256]{3,2,1,0:T(2,128)(2,1)S(1)}, bf16[64,4,1,256]{3,2,1,0:T(2,128)(2,1)S(1)}, u32[]{:S(2)}, u32[]{:S(2)}) collective-permute-start(bf16[64,4,1,256]{3,2,1,0:T(2,128)(2,1)S(1)} %get-tuple-element.260), channel_id=1, source_target_pairs={{1,0},{3,2},{5,4},{7,6},{9,8},{11,10},{13,12},{15,14},{17,16},{19,... | collective-permute-start | bytes 393224 | tf_op jit(solution)/shard_map/ppermute | solution.py:17
  171.3 267.6 %all-reduce.10.cloned.1.call-start = ((), (), s32[]{:S(2)}) async-start(), calls=%async_computation.3 | async-start | bytes 1769472 | tf_op jit(solution)/shard_map/psum | solution.py:154
  191.8 71.4 %copy-start.72 = (bf16[3,64,64]{2,1,0:T(8,128)(2,1)S(1)}, bf16[3,64,64]{2,1,0:T(8,128)(2,1)}, u32[]{:S(2)}) copy-start(bf16[3,64,64]{2,1,0:T(8,128)(2,1)} %rev.97) | copy-start | bytes 73732
  192.1 71.5 %copy-start.71 = (bf16[3,64,64]{2,1,0:T(8,128)(2,1)S(1)}, bf16[3,64,64]{2,1,0:T(8,128)(2,1)}, u32[]{:S(2)}) copy-start(bf16[3,64,64]{2,1,0:T(8,128)(2,1)} %rev.98) | copy-start | bytes 73732
  (75 other events, 420.5 us)
Sparse Core Ops, SparseCore 0:
  164.4 98.6 all-reduce.7
  268.5 131.7 all-reduce.11
  402.6 36.2 all-reduce.9
